TPU v7x, 128 devices: a whole 4x4x4 slice. The times are simulated.
128 devices in a mesh: comp: 16 (over x_lo, y, core), pair: 8 (over z, x_hi).
Axes of the slice: x: 4 (x_hi: 2, x_lo: 2; x = x_hi * 2 + x_lo), y: 4, z: 4, core: 2. Of those that a mesh axis runs over, the one named last changes fastest.
Arguments:
- densities: bfloat16 [8192, 65536], P('comp', 'pair'), may hold values from -6 to 6
- coulomb: float32 [8192], replicated, may hold values from 3.314563e-05 to 0.003314563
- pair_list: int32 [1024, 2], P(('comp', 'pair')), may hold values from 0 to 4095
- valence_energy: float32 [4096], replicated, may hold values from -20 to -0.5, as said below
- conduction_energy: float32 [4096], replicated, may hold values from 0.5 to 12, as said below
- tile_mask: int32 [512, 16], P(('pair', 'comp')), may hold values 0 or 1
Outputs:
- kernel: float32 [65536, 1024], P(('pair', 'comp'))
Inputs may be any that keep to these rules, and one draw needn't show every extreme that they name: `valence_energy`: energies in electronvolts. `conduction_energy`: energies in electronvolts.
All inputs are finite; a program needn't handle non-finite values. No bound on the sum of `tile_mask` on one device may be relied on, other than what follows from the above.
Results may differ from a plain program's by a relative error of at most 0.0025.
Values may be sent and summed in bfloat16 or wider, within the bound.
No kernel may reach another device: no remote copies, remote signals or barrier semaphores. Data moves between devices by JAX's collectives and lax.ppermute only.
A program may use at most 128 MiB of HBM per device.

v0:
```python
import jax
import jax.numpy as jnp
from jax import lax
from jax.sharding import PartitionSpec as P

TILE = 128


def per_device(densities, coulomb, pair_list, valence_energy, conduction_energy, tile_mask):
    comp_count = lax.axis_size("comp")
    pair_count = lax.axis_size("pair")
    comp_index = lax.axis_index("comp")
    pair_index = lax.axis_index("pair")
    block_len = densities.shape[0]
    pair_dev = densities.shape[1] // comp_count
    row_dev = pair_list.shape[0]
    window = row_dev * comp_count * pair_count
    weights = lax.dynamic_slice_in_dim(coulomb, comp_index * block_len, block_len)
    picked = densities.reshape(block_len, comp_count, pair_dev)[:, :, :row_dev]
    local_panel = (jnp.transpose(picked, (1, 2, 0)).astype(jnp.float32) * weights).astype(
        jnp.bfloat16
    )
    gathered = lax.all_gather(local_panel, "pair", axis=1, tiled=True)
    panel = gathered.reshape(window, block_len)
    exchange = lax.psum_scatter(
        lax.dot_general(
            densities, panel, (((0,), (1,)), ((), ())), preferred_element_type=jnp.float32
        ),
        "comp",
        scatter_dimension=0,
        tiled=True,
    )
    masked = (
        exchange.reshape(pair_dev // TILE, TILE, comp_count, window // comp_count)
        * tile_mask.astype(jnp.float32)[:, None, :, None]
    )
    masked = 2.0 * masked.reshape(pair_dev, window)
    table = jnp.arange(valence_energy.shape[0], dtype=jnp.int32)
    cond_hits = pair_list[:, 1][:, None] == table[None, :]
    val_hits = pair_list[:, 0][:, None] == table[None, :]
    energy = jnp.sum(jnp.where(cond_hits, conduction_energy[None, :], 0.0), axis=1) - jnp.sum(
        jnp.where(val_hits, valence_energy[None, :], 0.0), axis=1
    )
    diag_block = jnp.eye(row_dev, dtype=jnp.float32) * energy[None, :]
    start = (comp_index * pair_count + pair_index) * row_dev
    placed = lax.dynamic_update_slice(
        jnp.zeros((pair_dev, window), jnp.float32), diag_block, (jnp.int32(0), start)
    )
    return masked + placed


def solution(mesh):
    return jax.shard_map(
        per_device,
        mesh=mesh,
        in_specs=(
            P("comp", "pair"),
            P(),
            P(("comp", "pair"), None),
            P(),
            P(),
            P(("pair", "comp"), None),
        ),
        out_specs=P(("pair", "comp"), None),
        check_vma=False,
    )
```

profile of v0, /device:TPU:0, one launch (start us, length us, event | category | flops | bytes accessed | tf_op | source)
XLA Modules:
  0.0 278.9 jit_solution(5608610415269672751)
XLA Ops:
  6.5 0.0 all-gather.2.cloned.1.call-start
  6.5 12.0 %copy.12 = bf16[512,8192]{0,1:T(8,128)(2,1)} copy(bf16[512,8192]{1,0:T(8,128)(2,1)} %param.6) | data formatting | bytes 16777216 | tf_op args[0]
  18.5 0.8 dynamic_slice.3
  19.3 1.6 fusion.1
  20.9 0.0 all-gather.2.cloned.1.call-update
  20.9 0.0 reduce-scatter.2.cloned.1.call-start
  20.9 48.0 %all-gather.2.cloned.1.call-done = bf16[16,64,512]{2,1,0:T(8,128)(2,1)} async-done(((bf16[16,8,512]{2,1,0:T(8,128)(2,1)}), bf16[16,64,512]{2,1,0:T(8,128)(2,1)}) %all-gather.2.cloned.1.call-update) | async-done | bytes 1048592 | tf_op jit(solution)/shard_map/all_gather | solution.py:23
  68.9 17.7 %convolution_bitcast_fusion = f32[8192,1024]{0,1:T(8,128)} fusion(bf16[1024,512]{1,0:T(8,128)(2,1)} %bitcast.22, bf16[512,8192]{1,0:T(8,128)(2,1)} %param.6), kind=kOutput, calls=%fused_computation | convolution fusion | flops 8589934592 | bytes 42991616 | tf_op jit(solution)/shard_map/dot_general | solution.py:26
  86.7 0.0 copy-start.3
  86.7 0.0 copy-start.4
  86.7 0.0 copy-start.1
  86.7 0.0 copy-start.2
  86.7 0.0 reduce-scatter.2.cloned.1.call-update
  86.7 0.6 copy-done.3
  87.4 0.1 copy.13
  87.5 0.0 copy-done.4
  87.5 0.0 copy-done.1
  87.5 0.0 copy-done.2
  87.5 0.2 select_reduce_fusion
  87.7 179.8 %reduce-scatter.2.cloned.1.call-done = f32[512,1024]{0,1:T(8,128)} async-done(((f32[8192,1024]{0,1:T(8,128)}), f32[512,1024]{0,1:T(8,128)}) %reduce-scatter.2.cloned.1.call-update) | async-done | bytes 2097168 | tf_op jit(solution)/shard_map/reduce_scatter | solution.py:25
  267.6 0.0 copy-start
  267.6 0.3 mul.48
  267.9 1.2 copy-done
  269.2 0.5 fusion
  269.7 0.1 select_add_fusion
  269.7 0.5 add.18
  270.2 1.8 copy.14
  (3 shorter events, 0.0 us)
Async XLA Ops:
  6.5 62.4 %all-gather.2.cloned.1.call-start = ((), (), s32[]{:S(2)}) async-start(), calls=%async_computation.1 | async-start | bytes 1179648 | tf_op jit(solution)/shard_map/all_gather | solution.py:23
  20.9 246.7 %reduce-scatter.2.cloned.1.call-start = ((), (), s32[]{:S(2)}) async-start(), calls=%async_computation.2 | async-start | bytes 35651584 | tf_op jit(solution)/shard_map/reduce_scatter | solution.py:25
  86.7 0.7 copy-start.3
  86.7 0.8 copy-start.4
  86.7 0.8 copy-start.1
  86.7 0.8 copy-start.2
  267.6 1.6 copy-start
Sparse Core Ops, SparseCore 0:
  21.0 47.8 all-gather.1
  86.9 180.6 reduce-scatter.1
where the time goes:
time: 279 us
  waiting for transfers between devices  228 us (82%)
  matrix products  17.7 us (6%)
  local copies, waits for them, and re-layouts  17.3 us (6%)
  between operations  13.5 us (5%)
    reduce_scatter x1, waiting for transfers between devices, per_device(): lax.psum_scatter(lax.dot_general(densities, panel, (((0,), (1,)), ((), ()...  180 us
    all_gather x1, waiting for transfers between devices, per_device(): gathered = lax.all_gather(local_panel, 'pair', axis=1, tiled=True)  48 us
    dot_general x1, matrix products, per_device(): lax.dot_general(densities, panel, (((0,), (1,)), ((), ())), preferred_ele...  17.7 us
    unnamed x11, local copies, waits for them, and re-layouts  13.9 us
  transfers between devices with their start and end apart: 2, of which 2 were waited for; matrix products, arithmetic and copies ran while one was open for 0% of the time, Pallas kernels for 0%

commit v1 on v0

--- a/solution.py
+++ b/solution.py
@@ -20,7 +20,12 @@
     local_panel = (jnp.transpose(picked, (1, 2, 0)).astype(jnp.float32) * weights).astype(
         jnp.bfloat16
     )
-    gathered = lax.all_gather(local_panel, "pair", axis=1, tiled=True)
+    gathered = jnp.concatenate(
+        lax.all_to_all(
+            jnp.stack([local_panel for _ in range(lax.axis_size("pair"))]), "pair", 0, 0
+        ),
+        axis=1,
+    )
     panel = gathered.reshape(window, block_len)
     exchange = lax.psum_scatter(
         lax.dot_general(

time: 279 us -> 255 us (0.914)
  waiting for transfers between devices: 228 us -> 179 us
  blocking collectives: 0 us -> 24.9 us
    all_gather x1 -> x0, waiting for transfers between devices: 48 us -> none  [per_device(): gathered = lax.all_gather(local_panel, 'pair', axis=1, tiled=True)]
    all_to_all x0 -> x1, blocking collectives: none -> 24.9 us  [per_device(): lax.all_to_all(jnp.stack([local_panel for _ in range(lax.axis_size('pair'...]
    unnamed x11 -> x10, local copies, waits for them, and re-layouts: 13.9 us -> 1.9 us
    reshape x0 -> x1, local copies, waits for them, and re-layouts: none -> 12 us  [per_device(): picked = densities.reshape(block_len, comp_count, pair_dev)[:, :, :row_dev]]
  transfers between devices with their start and end apart: 2 -> 1, of which waited for: 2 -> 1; matrix products, arithmetic and copies ran while one was open for 0% -> 0% of each run, Pallas kernels for 0% -> 0%
where the time goes in v1:
time: 255 us
  waiting for transfers between devices  179 us (70%)
  blocking collectives  24.9 us (10%)
  matrix products  17.8 us (7%)
  local copies, waits for them, and re-layouts  17.5 us (7%)
  between operations  13.5 us (5%)
    reduce_scatter x1, waiting for transfers between devices, per_device(): lax.psum_scatter(lax.dot_general(densities, panel, (((0,), (1,)), ((), ()...  179 us
    all_to_all x1, blocking collectives, per_device(): lax.all_to_all(jnp.stack([local_panel for _ in range(lax.axis_size('pair'...  24.9 us
    dot_general x1, matrix products, per_device(): lax.dot_general(densities, panel, (((0,), (1,)), ((), ())), preferred_ele...  17.8 us
    reshape x1, local copies, waits for them, and re-layouts, per_device(): picked = densities.reshape(block_len, comp_count, pair_dev)[:, :, :row_dev]  12 us
  transfers between devices with their start and end apart: 1, of which 1 were waited for; matrix products, arithmetic and copies ran while one was open for 0% of the time, Pallas kernels for 0%

profile of v1, /device:TPU:0, one launch (start us, length us, event | category | flops | bytes accessed | tf_op | source)
XLA Modules:
  0.0 254.6 jit_solution(14417251003131686145)
XLA Ops:
  6.5 0.0 reduce-scatter.2.cloned.1.call-start
  6.5 12.0 %copy.21 = bf16[512,8192]{0,1:T(8,128)(2,1)} copy(bf16[512,8192]{1,0:T(8,128)(2,1)} %param.6) | data formatting | bytes 16777216 | tf_op jit(solution)/shard_map/reshape | solution.py:19
  18.5 0.8 dynamic_slice.3
  19.3 0.9 fusion.1
  20.2 0.1 stack.2
  20.3 24.9 %all_to_all.5 = bf16[8,16,8,512]{3,2,1,0:T(8,128)(2,1)S(1)} all-to-all(bf16[8,16,8,512]{3,2,1,0:T(8,128)(2,1)S(1)} %stack.2), channel_id=1, replica_groups=mesh['comp'=16,'pair'=8] {'pair'}, dimensions={0} | all-to-all | bytes 2097152 | tf_op jit(solution)/shard_map/all_to_all | solution.py:24
  45.1 0.1 copy.18
  45.2 17.8 %convolution_bitcast_fusion = f32[8192,1024]{0,1:T(8,128)} fusion(bf16[1024,512]{1,0:T(8,128)(2,1)S(1)} %bitcast.24, bf16[512,8192]{1,0:T(8,128)(2,1)} %param.6), kind=kOutput, calls=%fused_computation | convolution fusion | flops 8589934592 | bytes 42991616 | tf_op jit(solution)/shard_map/dot_general | solution.py:31
  63.1 0.0 copy-start.3
  63.1 0.0 copy-start.4
  63.1 0.0 copy-start.1
  63.1 0.0 copy-start.2
  63.1 0.0 reduce-scatter.2.cloned.1.call-update
  63.1 0.6 copy-done.3
  63.8 0.1 copy.19
  63.8 0.0 copy-done.4
  63.9 0.0 copy-done.1
  63.9 0.0 copy-done.2
  63.9 0.2 select_reduce_fusion
  64.1 179.1 %reduce-scatter.2.cloned.1.call-done = f32[512,1024]{0,1:T(8,128)} async-done(((f32[8192,1024]{0,1:T(8,128)}), f32[512,1024]{0,1:T(8,128)}) %reduce-scatter.2.cloned.1.call-update) | async-done | bytes 2097168 | tf_op jit(solution)/shard_map/reduce_scatter | solution.py:30
  243.3 0.0 copy-start
  243.3 0.3 mul.48
  243.6 1.2 copy-done
  244.9 0.5 fusion
  245.4 0.1 select_add_fusion
  245.4 0.5 add.18
  245.9 1.8 copy.20
  (3 shorter events, 0.0 us)
Async XLA Ops:
  6.5 236.7 %reduce-scatter.2.cloned.1.call-start = ((), (), s32[]{:S(2)}) async-start(), calls=%async_computation.2 | async-start | bytes 35651584 | tf_op jit(solution)/shard_map/reduce_scatter | solution.py:30
  63.1 0.7 copy-start.3
  63.1 0.8 copy-start.4
  63.1 0.8 copy-start.1
  63.1 0.8 copy-start.2
  243.3 1.6 copy-start
Sparse Core Ops, SparseCore 0:
  63.2 179.9 reduce-scatter.1
